TPU v7x, 32 devices: a whole 2x2x4 slice. The times are simulated.
32 devices in a mesh: dp: 8 (over z, x), seq: 4 (over y, core).
Axes of the slice: x: 2, y: 2, z: 4, core: 2. Of those that a mesh axis runs over, the one named last changes fastest.
Arguments:
- layer_in: bfloat16 [8192, 2048], P(('dp', 'seq')), may hold values from -6 to 6
- out_grad: bfloat16 [8192, 2048], P(('dp', 'seq')), may hold values from -6 to 6
- seq_start: int32 [8, 4], P('dp'), may hold values from 0 to 1, as said below
- norm1_gain: bfloat16 [2048], P(('dp', 'seq')), may hold values from 0.25 to 1.75
- norm1_shift: bfloat16 [2048], P(('dp', 'seq')), may hold values from -3 to 3
- proj_in: bfloat16 [2048, 12288], P(('dp', 'seq')), may hold values from -0.125 to 0.125
- proj_out: bfloat16 [4096, 2048], P(('dp', 'seq')), may hold values from -0.125 to 0.125
- norm2_gain: bfloat16 [2048], P(('dp', 'seq')), may hold values from 0.25 to 1.75
- norm2_shift: bfloat16 [2048], P(('dp', 'seq')), may hold values from -3 to 3
- ffn_up: bfloat16 [2048, 4096], P(('dp', 'seq')), may hold values from -0.125 to 0.125
- ffn_down: bfloat16 [4096, 2048], P(('dp', 'seq')), may hold values from -0.125 to 0.125
Outputs:
- layer_out: bfloat16 [8192, 2048], P(('dp', 'seq'))
- in_grad: bfloat16 [8192, 2048], P(('dp', 'seq'))
- norm1_gain_grad: float32 [2048], P(('dp', 'seq'))
- norm1_shift_grad: float32 [2048], P(('dp', 'seq'))
- proj_in_grad: float32 [2048, 12288], P(('dp', 'seq'))
- proj_out_grad: float32 [4096, 2048], P(('dp', 'seq'))
- norm2_gain_grad: float32 [2048], P(('dp', 'seq'))
- norm2_shift_grad: float32 [2048], P(('dp', 'seq'))
- ffn_up_grad: float32 [2048, 4096], P(('dp', 'seq'))
- ffn_down_grad: float32 [4096, 2048], P(('dp', 'seq'))
Inputs may be any that keep to these rules, and one draw needn't show every extreme that they name: `seq_start`: each group's first block is 1, and a 1 stands only at even block indices, so every sequence covers an even number of blocks of 256 tokens.
All inputs are finite; a program needn't handle non-finite values.
Results may differ from a plain program's by a relative error of at most 0.014.
The roundings to bfloat16 on the way count: a program that leaves them out, or rounds other values in their place, can miss the bound.
Values may be sent and summed in bfloat16 or wider, within the bound.
No kernel may reach another device: no remote copies, remote signals or barrier semaphores. Data moves between devices by JAX's collectives and lax.ppermute only.
A program may use at most 336 MiB of HBM per device.

v0:
```python
import jax
import jax.numpy as jnp
from jax import lax
from jax.sharding import PartitionSpec as P

D = 2048
HEADS = 8
VD = 4096
DK = 256
DV = 512
BOTH = ("dp", "seq")
f32 = jnp.float32
bf16 = jnp.bfloat16


def layer_norm(rows, row_gain, row_shift):
    average = jnp.mean(rows, axis=-1, keepdims=True)
    centred = rows - average
    spread = jnp.mean(centred * centred, axis=-1, keepdims=True)
    return centred * lax.rsqrt(spread + 1e-05) * row_gain + row_shift


def gate_norm(gate_pre, retained):
    average = jnp.mean(retained, axis=-1, keepdims=True)
    centred = retained - average
    spread = jnp.maximum(jnp.mean(centred * centred, axis=-1, keepdims=True), 0.25)
    normed = centred * lax.rsqrt(spread + 1e-05)
    swish = gate_pre * jax.nn.sigmoid(gate_pre)
    return swish * normed


def gelu_exact(values):
    return jax.nn.gelu(values, approximate=False)


def rotate(heads_in, cosine, sine):
    half_width = heads_in.shape[-1] // 2
    first = heads_in[..., :half_width]
    second = heads_in[..., half_width:]
    return jnp.concatenate(
        [first * cosine - second * sine, first * sine + second * cosine], axis=-1
    )


def dot(a, b, dims):
    return lax.dot_general(a, b, (dims, ((), ())), preferred_element_type=f32)


def seq_bits(size):
    return [1 << b for b in range(size.bit_length() - 1)]


def swap_seq(x, bit):
    size = lax.axis_size("seq")
    return lax.ppermute(x, "seq", [(i, i ^ bit) for i in range(size)])


def gather_seq(x):
    size, me = (lax.axis_size("seq"), lax.axis_index("seq"))
    held = x[None]
    for bit in reversed(seq_bits(size)):
        other = swap_seq(held, bit)
        upper = me & bit != 0
        held = jnp.where(upper, jnp.stack([other, held]), jnp.stack([held, other]))
        held = held.reshape((-1,) + x.shape) if bit == size // 2 else held
        if bit != size // 2:
            held = jnp.swapaxes(held, 0, 1).reshape((-1,) + x.shape)
    return held


def scatter_seq(x):
    size, me = (lax.axis_size("seq"), lax.axis_index("seq"))
    held = x
    for bit in seq_bits(size):
        pairs = held.reshape((held.shape[0] // 2, 2) + held.shape[1:])
        mine = jnp.where(me & bit != 0, 1, 0)
        keep = lax.dynamic_index_in_dim(pairs, mine, 1, False)
        give = lax.dynamic_index_in_dim(pairs, 1 - mine, 1, False)
        held = keep.astype(f32) + swap_seq(give.astype(bf16), bit).astype(f32)
    return held[0]


def exchange_seq(x):
    return lax.all_to_all(x, "seq", 0, 0)


def gather_dp(x):
    return lax.all_gather(x, "dp", axis=0, tiled=True)


def scatter_dp(x):
    return lax.psum_scatter(x.astype(bf16), "dp", scatter_dimension=0, tiled=True)


def local(
    layer_in,
    out_grad,
    seq_start,
    norm1_gain,
    norm1_shift,
    proj_in,
    proj_out,
    norm2_gain,
    norm2_shift,
    ffn_up,
    ffn_down,
):
    S, G = (lax.axis_size("seq"), lax.axis_size("dp"))
    me = lax.axis_index("seq")
    T = layer_in.shape[0]
    TG = S * T
    H = HEADS // S
    QW, VW = (H * DK, H * DV)
    FR = ffn_down.shape[0]
    FW = G * FR
    norms = lax.all_gather(
        jnp.stack([norm1_gain, norm1_shift, norm2_gain, norm2_shift]), BOTH, axis=1, tiled=True
    ).astype(f32)
    gain_one, shift_one, gain_two, shift_two = norms
    rows_in = proj_in.shape[0]
    pieces = []
    start = 0
    for width in (QW, QW, VW, VW):
        part = proj_in[:, start : start + S * width]
        pieces.append(part.reshape(rows_in, S, width))
        start += S * width
    w_in = jnp.concatenate(pieces, axis=2).transpose(1, 0, 2)
    w_in = exchange_seq(w_in).reshape(S * rows_in, 2 * QW + 2 * VW)
    w_in = gather_dp(w_in)
    w_out = lax.ppermute(
        proj_out, BOTH, [(j * G + t, t * S + j) for j in range(S) for t in range(G)]
    )
    w_out = gather_dp(w_out)
    rows_up = ffn_up.shape[0]
    w_up = ffn_up.reshape(rows_up, G, S, FR).transpose(2, 0, 1, 3).reshape(S, rows_up, FW)
    w_up = gather_dp(exchange_seq(w_up).reshape(S * rows_up, FW))
    w_down = gather_dp(ffn_down)
    rows_full = layer_in.astype(f32)
    normed_one, norm1_back = jax.vjp(layer_norm, rows_full, gain_one, shift_one)
    hidden_one = gather_seq(normed_one.astype(bf16)).reshape(TG, D)
    cot = gather_seq(out_grad).reshape(TG, D)
    projected = dot(hidden_one, w_in, ((1,), (0,)))
    q_pre = projected[:, :QW].reshape(S, T, H, DK)
    k_pre = projected[:, QW : 2 * QW].reshape(S, T, H, DK)
    values = projected[:, 2 * QW : 2 * QW + VW].astype(bf16).reshape(S, T, H, DV)
    gate_pre = projected[:, 2 * QW + VW :].reshape(S, T, H, DV)
    half = DK // 2
    factor = jnp.power(10000.0, -jnp.arange(half, dtype=f32) / (half - 1))
    angles = jnp.arange(TG, dtype=f32)[:, None] * factor[None, :]
    cosine = jnp.cos(angles).reshape(S, T, 1, half)
    sine = jnp.sin(angles).reshape(S, T, 1, half)
    key_scale = DK ** (-0.5)
    queries = rotate(q_pre, cosine, sine).astype(bf16)
    keys = (rotate(k_pre, cosine, sine) * key_scale).astype(bf16)
    log_all = jnp.log(1.0 - jnp.exp2(-5.0 - jnp.arange(HEADS, dtype=f32)))
    log_decay = lax.dynamic_slice_in_dim(log_all, me * H, H)
    steps = jnp.arange(T, dtype=f32)
    decay_query = jnp.exp((steps + 1.0)[:, None] * log_decay[None, :])
    decay_key = jnp.exp((T - 1.0 - steps)[:, None] * log_decay[None, :])
    distance = steps[:, None] - steps[None, :]
    lower = distance[None] >= 0.0
    safe = jnp.where(lower, distance[None], 0.0)
    mask = jnp.where(lower, jnp.exp(safe * log_decay[:, None, None]), 0.0)
    block_decay = jnp.exp(T * log_decay)[:, None, None]
    keep = 1.0 - seq_start[0].astype(f32)
    query_decay = (queries.astype(f32) * decay_query[None, :, :, None]).astype(bf16)
    key_decay = (keys.astype(f32) * decay_key[None, :, :, None]).astype(bf16)

    def ein(spec, a, b):
        return jnp.einsum(spec, a, b, preferred_element_type=f32)

    raw = ein("bihd,bjhd->bhij", queries, keys)
    scores = (raw * mask[None]).astype(bf16)
    local_state = ein("bjhd,bjhe->bhde", key_decay, values)
    carry = jnp.zeros_like(local_state[0])
    states = []
    for b in range(S):
        state = keep[b] * carry
        states.append(state.astype(bf16))
        carry = block_decay * state + local_state[b]
    state_in = jnp.stack(states)
    retained = ein("bhij,bjhe->bihe", scores, values) + ein(
        "bihd,bhde->bihe", query_decay, state_in
    )
    gated, gate_back = jax.vjp(gate_norm, gate_pre, retained)
    mixed = gated.astype(bf16).reshape(TG, VW)
    attn = scatter_seq(dot(mixed, w_out, ((1,), (0,))).reshape(S, T, D))
    middle = rows_full + attn
    normed_two, norm2_back = jax.vjp(layer_norm, middle, gain_two, shift_two)
    hidden_two = gather_seq(normed_two.astype(bf16)).reshape(TG, D)
    up_pre = dot(hidden_two, w_up, ((1,), (0,)))
    active_full, gelu_back = jax.vjp(gelu_exact, up_pre)
    active = active_full.astype(bf16)
    down = scatter_seq(dot(active, w_down, ((1,), (0,))).reshape(S, T, D))
    layer_out = (middle + down).astype(bf16)
    down_grad = scatter_dp(dot(active, cot, ((0,), (0,)))).astype(f32)
    grad_active = dot(cot, w_down, ((1,), (1,)))
    grad_up = gelu_back(grad_active)[0].astype(bf16)
    up_grad = scatter_dp(dot(hidden_two, grad_up, ((0,), (0,))))
    up_grad = exchange_seq(up_grad.reshape(S, rows_up, FW)).reshape(S, rows_up, G, FR)
    up_grad = up_grad.transpose(1, 2, 0, 3).reshape(rows_up, G * S * FR).astype(f32)
    grad_hidden_two = scatter_seq(dot(grad_up, w_up, ((1,), (1,))).reshape(S, T, D))
    grad_mid_part, gain_two_grad, shift_two_grad = norm2_back(grad_hidden_two)
    grad_middle = out_grad.astype(f32) + grad_mid_part
    grad_attn = gather_seq(grad_middle.astype(bf16)).reshape(TG, D)
    out_term = scatter_dp(dot(mixed, grad_attn, ((0,), (0,))))
    out_grad_w = lax.ppermute(
        out_term, BOTH, [(t * S + j, j * G + t) for j in range(S) for t in range(G)]
    ).astype(f32)
    grad_mixed = dot(grad_attn, w_out, ((1,), (1,))).reshape(S, T, H, DV)
    grad_gate, grad_ret = gate_back(grad_mixed)
    grad_gate = grad_gate.astype(bf16)
    grad_ret = grad_ret.astype(bf16)
    grad_qdecay = ein("bihe,bhde->bihd", grad_ret, state_in)
    state_grad = ein("bihd,bihe->bhde", query_decay, grad_ret)
    grad_scores = ein("bihe,bjhe->bhij", grad_ret, values)
    grad_raw = (grad_scores * mask[None]).astype(bf16)
    later = jnp.zeros_like(state_grad[0])
    laters = [None] * S
    for b in reversed(range(S)):
        laters[b] = later.astype(bf16)
        later = keep[b] * (state_grad[b] + block_decay * later)
    grad_local = jnp.stack(laters)
    grad_query = (
        ein("bhij,bjhd->bihd", grad_raw, keys) + grad_qdecay * decay_query[None, :, :, None]
    )
    grad_key = (
        ein("bhij,bihd->bjhd", grad_raw, queries)
        + ein("bjhe,bhde->bjhd", values, grad_local) * decay_key[None, :, :, None]
    )
    grad_value = ein("bhij,bihe->bjhe", scores, grad_ret) + ein(
        "bjhd,bhde->bjhe", key_decay, grad_local
    )
    grad_qpre = rotate(grad_query, cosine, -sine).astype(bf16).reshape(TG, QW)
    grad_kpre = rotate(grad_key * key_scale, cosine, -sine).astype(bf16).reshape(TG, QW)
    grad_projected = jnp.concatenate(
        [grad_qpre, grad_kpre, grad_value.astype(bf16).reshape(TG, VW), grad_gate.reshape(TG, VW)],
        axis=1,
    )
    in_term = scatter_dp(dot(hidden_one, grad_projected, ((0,), (0,))))
    in_term = exchange_seq(in_term.reshape(S, rows_in, 2 * QW + 2 * VW))
    cols = []
    start = 0
    for width in (QW, QW, VW, VW):
        part = in_term[:, :, start : start + width]
        cols.append(part.transpose(1, 0, 2).reshape(rows_in, S * width))
        start += width
    in_grad_w = jnp.concatenate(cols, axis=1).astype(f32)
    grad_hidden_one = scatter_seq(dot(grad_projected, w_in, ((1,), (1,))).reshape(S, T, D))
    grad_in_part, gain_one_grad, shift_one_grad = norm1_back(grad_hidden_one)
    in_grad = (grad_middle + grad_in_part).astype(bf16)
    norm_grads = lax.psum_scatter(
        jnp.stack([gain_one_grad, shift_one_grad, gain_two_grad, shift_two_grad]),
        BOTH,
        scatter_dimension=1,
        tiled=True,
    )
    return (
        layer_out,
        in_grad,
        norm_grads[0],
        norm_grads[1],
        in_grad_w,
        out_grad_w,
        norm_grads[2],
        norm_grads[3],
        up_grad,
        down_grad,
    )


def solution(mesh):
    rows, vector = (P(BOTH, None), P(BOTH))
    in_specs = (rows, rows, P("dp", None), vector, vector, rows, rows, vector, vector, rows, rows)
    out_specs = (rows, rows, vector, vector, rows, rows, vector, vector, rows, rows)
    return jax.shard_map(local, mesh=mesh, in_specs=in_specs, out_specs=out_specs, check_vma=False)
```

profile of v0, /device:TPU:0, one launch (start us, length us, event | category | flops | bytes accessed | tf_op | source)
XLA Modules:
  0.0 1129.7 jit_solution(7035085313268230148)
XLA Ops:
  12.0 24.4 %all_to_all.20 = bf16[4,64,3072]{2,1,0:T(8,128)(2,1)} all-to-all(bf16[4,64,3072]{2,1,0:T(8,128)(2,1)S(1)} %copy.198), channel_id=1, replica_groups=mesh['dp'=8,'seq'=4] {'seq'}, dimensions={0} | all-to-all | bytes 3145728 | tf_op jit(solution)/shard_map/all_to_all | solution.py:84
  38.0 106.0 %all-gather = bf16[32,64,4]{1,2,0:T(4,128)(2,1)S(1)} all-gather(bf16[1,64,4]{1,2,0:T(4,128)(2,1)S(1)} %maximum_bitcast_fusion.1), channel_id=1, replica_groups=mesh['dp'=8,'seq'=4] {'dp','seq'}, dimensions={0}, use_global_device_ids=true | all-gather | bytes 16896 | tf_op jit(solution)/shard_map/all_gather | solution.py:116
  157.3 15.8 %collective-permute-done = bf16[1,256,2048]{2,1,0:T(8,128)(2,1)S(1)} collective-permute-done((bf16[1,256,2048]{2,1,0:T(8,128)(2,1)}, bf16[1,256,2048]{2,1,0:T(8,128)(2,1)S(1)}, u32[]{:S(2)}, u32[]{:S(2)}) %collective-permute-start) | collective-permute-done | bytes 1048608 | tf_op jit(solution)/shard_map/ppermute | solution.py:55
  188.4 51.1 %all-gather.6.cloned.1.call-done = bf16[2048,3072]{1,0:T(8,128)(2,1)} async-done(((bf16[256,3072]{1,0:T(8,128)(2,1)}), bf16[2048,3072]{1,0:T(8,128)(2,1)}) %all-gather.6.cloned.1.call-update) | async-done | bytes 12582928 | tf_op jit(solution)/shard_map/all_gather | solution.py:88
  239.5 17.0 %fusion.85 = f32[1024,3072]{1,0:T(8,128)S(1)} fusion(bf16[1024,2048]{1,0:T(8,128)(2,1)} %bitcast.265, bf16[2048,3072]{1,0:T(8,128)(2,1)} %all-gather.6.cloned.1.call-done), kind=kOutput, calls=%fused_computation.220 | convolution fusion | flops 12884901888 | bytes 29360128 | tf_op jit(solution)/shard_map/dot_general | solution.py:46
  270.5 6.7 reshape.732
  277.2 7.2 copy.200
  303.1 10.7 all-gather.8.cloned.1.call-done
  313.8 6.4 fusion.8
  335.7 23.9 %collective-permute-done.4 = bf16[1,256,2048]{2,1,0:T(8,128)(2,1)} collective-permute-done((bf16[1,256,2048]{2,1,0:T(8,128)(2,1)S(1)}, bf16[1,256,2048]{2,1,0:T(8,128)(2,1)}, u32[]{:S(2)}, u32[]{:S(2)}) %collective-permute-start.4) | collective-permute-done | bytes 1048608 | tf_op jit(solution)/shard_map/ppermute | solution.py:55
  364.4 17.7 %collective-permute-done.9 = bf16[1,256,2048]{2,1,0:T(8,128)(2,1)S(1)} collective-permute-done((bf16[1,256,2048]{2,1,0:T(8,128)(2,1)}, bf16[1,256,2048]{2,1,0:T(8,128)(2,1)S(1)}, u32[]{:S(2)}, u32[]{:S(2)}) %collective-permute-start.9) | collective-permute-done | bytes 1048608 | tf_op jit(solution)/shard_map/ppermute | solution.py:55
  384.1 19.6 %collective-permute-done.5 = bf16[1,256,2048]{2,1,0:T(8,128)(2,1)S(1)} collective-permute-done((bf16[1,256,2048]{2,1,0:T(8,128)(2,1)S(1)}, bf16[1,256,2048]{2,1,0:T(8,128)(2,1)S(1)}, u32[]{:S(2)}, u32[]{:S(2)}) %collective-permute-start.5) | collective-permute-done | bytes 1048608 | tf_op jit(solution)/shard_map/ppermute | solution.py:55
  413.4 9.9 fusion.86
  423.2 38.1 %all-gather.12.cloned.1.call-done = bf16[1024,2048]{1,0:T(8,128)(2,1)} async-done(((bf16[128,2048]{1,0:T(8,128)(2,1)}), bf16[1024,2048]{1,0:T(8,128)(2,1)}) %all-gather.12.cloned.1.call-update) | async-done | bytes 4194320 | tf_op jit(solution)/shard_map/all_gather | solution.py:88
  461.3 16.9 %add_convert_fusion.2 = (bf16[1024,1024]{1,0:T(8,128)(2,1)S(1)}, f32[1024,1024]{1,0:T(8,128)S(1)}) fusion(f32[1024,1024]{1,0:T(8,128)} %fusion.86, bf16[1024,2048]{1,0:T(8,128)(2,1)} %bitcast.269, bf16[1024,2048]{1,0:T(8,128)(2,1)} %all-gather.12.cloned.1.call-done), kind=kOutput, calls=%fused_computation.31 | convolution fusion | flops 4370464768 | bytes 18874368 | tf_op jit(solution)/shard_map/dot_general | solution.py:46
  481.9 6.2 convolution_convert_fusion.2
  488.2 7.3 fusion.88
  510.5 18.6 %collective-permute-done.12 = bf16[1,256,2048]{2,1,0:T(8,128)(2,1)S(1)} collective-permute-done((bf16[1,256,2048]{2,1,0:T(8,128)(2,1)S(1)}, bf16[1,256,2048]{2,1,0:T(8,128)(2,1)S(1)}, u32[]{:S(2)}, u32[]{:S(2)}) %collective-permute-start.12) | collective-permute-done | bytes 1048608 | tf_op jit(solution)/shard_map/ppermute | solution.py:55
  529.9 21.3 %collective-permute-done.8 = bf16[1,256,2048]{2,1,0:T(8,128)(2,1)S(1)} collective-permute-done((bf16[1,256,2048]{2,1,0:T(8,128)(2,1)S(1)}, bf16[1,256,2048]{2,1,0:T(8,128)(2,1)S(1)}, u32[]{:S(2)}, u32[]{:S(2)}) %collective-permute-start.8) | collective-permute-done | bytes 1048608 | tf_op jit(solution)/shard_map/ppermute | solution.py:55
  557.0 23.3 %collective-permute-done.13 = bf16[1,256,2048]{2,1,0:T(8,128)(2,1)S(1)} collective-permute-done((bf16[1,256,2048]{2,1,0:T(8,128)(2,1)S(1)}, bf16[1,256,2048]{2,1,0:T(8,128)(2,1)S(1)}, u32[]{:S(2)}, u32[]{:S(2)}) %collective-permute-start.13) | collective-permute-done | bytes 1048608 | tf_op jit(solution)/shard_map/ppermute | solution.py:55
  582.1 6.4 convolution_convert_fusion.1
  600.1 5.3 multiply_reduce_fusion
  610.0 6.6 copy.235
  638.1 6.3 copy.232
  653.1 16.0 %convolution_convert_fusion = bf16[2048,3072]{1,0:T(8,128)(2,1)} fusion(bf16[1024,2048]{1,0:T(8,128)(2,1)S(1)} %bitcast.266, bf16[1024,3072]{1,0:T(8,128)(2,1)S(1)} %constant_dynamic-update-slice_fusion), kind=kOutput, calls=%fused_computation | convolution fusion | flops 12891193344 | bytes 23068672 | tf_op jit(solution)/shard_map/dot_general | solution.py:46
  669.2 6.2 copy.241
  678.2 6.2 convolution_convert_fusion.3
  684.4 18.0 %fusion.90 = f32[1024,2048]{1,0:T(8,128)S(1)} fusion(bf16[1024,3072]{1,0:T(8,128)(2,1)} %copy-done.48, bf16[2048,3072]{1,0:T(8,128)(2,1)} %all-gather.6.cloned.1.call-done), kind=kOutput, calls=%fused_computation.225 | convolution fusion | flops 12884901888 | bytes 27262976 | tf_op jit(solution)/shard_map/dot_general | solution.py:46
  721.2 21.4 %all-to-all-done.3 = bf16[4,64,1024]{2,1,0:T(8,128)(2,1)} async-done(((bf16[4,64,1024]{2,1,0:T(8,128)(2,1)}), bf16[4,64,1024]{2,1,0:T(8,128)(2,1)}, u32[]{:S(2)}, u32[]{:S(2)}) %all-to-all-start.3) | async-done | bytes 524320 | tf_op jit(solution)/shard_map/all_to_all | solution.py:84
  752.4 133.5 %reduce-scatter.8.cloned.1.call-done = bf16[256,3072]{1,0:T(8,128)(2,1)} async-done(((bf16[2048,3072]{1,0:T(8,128)(2,1)}), bf16[256,3072]{1,0:T(8,128)(2,1)}) %reduce-scatter.8.cloned.1.call-update) | async-done | bytes 1572880 | tf_op jit(solution)/shard_map/reduce_scatter | solution.py:92
  894.2 82.5 %reduce-scatter.10.cloned.1.call-done = bf16[128,2048]{1,0:T(8,128)(2,1)} async-done(((bf16[1024,2048]{1,0:T(8,128)(2,1)}), bf16[128,2048]{1,0:T(8,128)(2,1)}) %reduce-scatter.10.cloned.1.call-update) | async-done | bytes 524304 | tf_op jit(solution)/shard_map/reduce_scatter | solution.py:92
  981.7 132.5 %reduce-scatter.16.cloned.1.call-done = f32[64,4]{1,0:T(8,128)} async-done(((f32[2048,4]{1,0:T(8,128)}), f32[64,4]{1,0:T(8,128)}) %reduce-scatter.16.cloned.1.call-update) | async-done | bytes 1040
  (353 shorter events, 224.6 us)
Async XLA Ops:
  7.2 232.3 %all-gather.6.cloned.1.call-start = ((), (), s32[]{:S(2)}) async-start(), calls=%async_computation.9 | async-start | bytes 14155776 | tf_op jit(solution)/shard_map/all_gather | solution.py:88
  12.0 132.2 %copy-start.4 = (bf16[256,2048]{1,0:T(8,128)(2,1)S(1)}, bf16[256,2048]{1,0:T(8,128)(2,1)}, u32[]{:S(2)}) copy-start(bf16[256,2048]{1,0:T(8,128)(2,1)} %param.11) | copy-start | bytes 3145732
  36.4 277.4 %all-gather.8.cloned.1.call-start = ((), (), s32[]{:S(2)}) async-start(), calls=%async_computation.10 | async-start | bytes 4718592 | tf_op jit(solution)/shard_map/all_gather | solution.py:88
  36.5 0.7 collective-permute-start.2
  146.9 26.2 %collective-permute-start = (bf16[1,256,2048]{2,1,0:T(8,128)(2,1)}, bf16[1,256,2048]{2,1,0:T(8,128)(2,1)S(1)}, u32[]{:S(2)}, u32[]{:S(2)}) collective-permute-start(bf16[1,256,2048]{2,1,0:T(8,128)(2,1)} %get-tuple-element.56), channel_id=1, source_target_pairs={{0,2},{1,3},{2,0},{3,1},{4,6},{5,7},{6,4},{7,5},{8,10},{9,11},{10,... | collective-permute-start | bytes 3145736 | tf_op jit(solution)/shard_map/ppermute | solution.py:55
  153.1 29.6 %all-to-all-start.1 = ((bf16[4,64,1024]{2,1,0:T(8,128)(2,1)}), bf16[4,64,1024]{2,1,0:T(8,128)(2,1)}, u32[]{:S(2)}, u32[]{:S(2)}) async-start(bf16[4,64,1024]{2,1,0:T(8,128)(2,1)} %reshape.737), calls=%async_computation.1 | async-start | bytes 1048576 | tf_op jit(solution)/shard_map/all_to_all | solution.py:84
  157.2 256.1 %all-gather.10.cloned.1.call-start = ((), (), s32[]{:S(2)}) async-start(), calls=%async_computation.11 | async-start | bytes 4718592 | tf_op jit(solution)/shard_map/all_gather | solution.py:88
  176.4 6.9 collective-permute-start.1
  178.5 118.1 %copy-start.51 = (f32[256,2]{0,1:T(2,128)}, f32[256,2]{0,1:T(2,128)S(1)}, u32[]{:S(2)}) copy-start(f32[256,2]{0,1:T(2,128)S(1)} %get-tuple-element.80) | copy-start | bytes 6148
  182.7 278.6 %all-gather.12.cloned.1.call-start = ((), (), s32[]{:S(2)}) async-start(), calls=%async_computation.12 | async-start | bytes 4718592 | tf_op jit(solution)/shard_map/all_gather | solution.py:88
  324.2 4.4 collective-permute-start.3
  333.5 26.2 %collective-permute-start.4 = (bf16[1,256,2048]{2,1,0:T(8,128)(2,1)S(1)}, bf16[1,256,2048]{2,1,0:T(8,128)(2,1)}, u32[]{:S(2)}, u32[]{:S(2)}) collective-permute-start(bf16[1,256,2048]{2,1,0:T(8,128)(2,1)S(1)} %dynamic-slice_convert_fusion.4), channel_id=1, source_target_pairs={{0,2},{1,3},{2,0},{3,1},{4,6},{5,7},{6,4},{7,5},{8,10},{9,11},{10,... | collective-permute-start | bytes 3145736 | tf_op jit(solution)/shard_map/ppermute | solution.py:55
  335.1 377.7 %reduce-scatter.12.cloned.1.call-start = ((), (), s32[]{:S(2)}) async-start(), calls=%async_computation.15 | async-start | bytes 4718592 | tf_op jit(solution)/shard_map/reduce_scatter | solution.py:92
  335.1 46.9 %collective-permute-start.9 = (bf16[1,256,2048]{2,1,0:T(8,128)(2,1)}, bf16[1,256,2048]{2,1,0:T(8,128)(2,1)S(1)}, u32[]{:S(2)}, u32[]{:S(2)}) collective-permute-start(bf16[1,256,2048]{2,1,0:T(8,128)(2,1)} %bitcast.42), channel_id=1, source_target_pairs={{0,2},{1,3},{2,0},{3,1},{4,6},{5,7},{6,4},{7,5},{8,10},{9,11},{10,... | collective-permute-start | bytes 3145736 | tf_op jit(solution)/shard_map/ppermute | solution.py:55
  362.9 40.9 %collective-permute-start.5 = (bf16[1,256,2048]{2,1,0:T(8,128)(2,1)S(1)}, bf16[1,256,2048]{2,1,0:T(8,128)(2,1)S(1)}, u32[]{:S(2)}, u32[]{:S(2)}) collective-permute-start(bf16[1,256,2048]{2,1,0:T(8,128)(2,1)S(1)} %fusion.126), channel_id=1, source_target_pairs={{0,2},{1,3},{2,0},{3,1},{4,6},{5,7},{6,4},{7,5},{8,10},{9,11},{10,... | collective-permute-start | bytes 3145736 | tf_op jit(solution)/shard_map/ppermute | solution.py:55
  384.0 22.1 %collective-permute-start.10 = (bf16[2,256,2048]{2,1,0:T(8,128)(2,1)S(1)}, bf16[2,256,2048]{2,1,0:T(8,128)(2,1)S(1)}, u32[]{:S(2)}, u32[]{:S(2)}) collective-permute-start(bf16[2,256,2048]{2,1,0:T(8,128)(2,1)S(1)} %maximum_select_fusion.8), channel_id=1, source_target_pairs={{0,1},{1,0},{2,3},{3,2},{4,5},{5,4},{6,7},{7,6},{8,9},{9,8},{10,11... | collective-permute-start | bytes 6291464 | tf_op jit(solution)/shard_map/ppermute | solution.py:55
  404.1 6.2 collective-permute-start.6
  488.1 230.9 %reduce-scatter.14.cloned.1.call-start = ((), (), s32[]{:S(2)}) async-start(), calls=%async_computation.16 | async-start | bytes 4718592 | tf_op jit(solution)/shard_map/reduce_scatter | solution.py:92
  495.9 6.2 collective-permute-start.11
  502.0 4.4 collective-permute-start.7
  503.1 26.0 %collective-permute-start.12 = (bf16[1,256,2048]{2,1,0:T(8,128)(2,1)S(1)}, bf16[1,256,2048]{2,1,0:T(8,128)(2,1)S(1)}, u32[]{:S(2)}, u32[]{:S(2)}) collective-permute-start(bf16[1,256,2048]{2,1,0:T(8,128)(2,1)S(1)} %dynamic-slice_convert_fusion.2), channel_id=1, source_target_pairs={{0,2},{1,3},{2,0},{3,1},{4,6},{5,7},{6,4},{7,5},{8,10},{9,11},{10,... | collective-permute-start | bytes 3145736 | tf_op jit(solution)/shard_map/ppermute | solution.py:55
  509.0 42.2 %collective-permute-start.8 = (bf16[1,256,2048]{2,1,0:T(8,128)(2,1)S(1)}, bf16[1,256,2048]{2,1,0:T(8,128)(2,1)S(1)}, u32[]{:S(2)}, u32[]{:S(2)}) collective-permute-start(bf16[1,256,2048]{2,1,0:T(8,128)(2,1)S(1)} %dynamic-slice_convert_fusion.3), channel_id=1, source_target_pairs={{0,2},{1,3},{2,0},{3,1},{4,6},{5,7},{6,4},{7,5},{8,10},{9,11},{10,... | collective-permute-start | bytes 3145736 | tf_op jit(solution)/shard_map/ppermute | solution.py:55
  555.5 24.8 %collective-permute-start.13 = (bf16[1,256,2048]{2,1,0:T(8,128)(2,1)S(1)}, bf16[1,256,2048]{2,1,0:T(8,128)(2,1)S(1)}, u32[]{:S(2)}, u32[]{:S(2)}) collective-permute-start(bf16[1,256,2048]{2,1,0:T(8,128)(2,1)S(1)} %fusion.124), channel_id=1, source_target_pairs={{0,2},{1,3},{2,0},{3,1},{4,6},{5,7},{6,4},{7,5},{8,10},{9,11},{10,... | collective-permute-start | bytes 3145736 | tf_op jit(solution)/shard_map/ppermute | solution.py:55
  582.0 10.0 collective-permute-start.14
  588.5 297.4 %reduce-scatter.8.cloned.1.call-start = ((), (), s32[]{:S(2)}) async-start(), calls=%async_computation.13 | async-start | bytes 14155776 | tf_op jit(solution)/shard_map/reduce_scatter | solution.py:92
  669.1 307.6 %reduce-scatter.10.cloned.1.call-start = ((), (), s32[]{:S(2)}) async-start(), calls=%async_computation.14 | async-start | bytes 4718592 | tf_op jit(solution)/shard_map/reduce_scatter | solution.py:92
  702.7 4.4 collective-permute-start.15
  711.3 34.6 %collective-permute-start.16 = (bf16[1,256,2048]{2,1,0:T(8,128)(2,1)}, bf16[1,256,2048]{2,1,0:T(8,128)(2,1)}, u32[]{:S(2)}, u32[]{:S(2)}) collective-permute-start(bf16[1,256,2048]{2,1,0:T(8,128)(2,1)} %dynamic-slice_convert_fusion.1), channel_id=1, source_target_pairs={{0,2},{1,3},{2,0},{3,1},{4,6},{5,7},{6,4},{7,5},{8,10},{9,11},{10,... | collective-permute-start | bytes 3145736 | tf_op jit(solution)/shard_map/ppermute | solution.py:55
  712.8 29.9 %all-to-all-start.3 = ((bf16[4,64,1024]{2,1,0:T(8,128)(2,1)}), bf16[4,64,1024]{2,1,0:T(8,128)(2,1)}, u32[]{:S(2)}, u32[]{:S(2)}) async-start(bf16[4,64,1024]{2,1,0:T(8,128)(2,1)} %bitcast.289), calls=%async_computation.6 | async-start | bytes 1048576 | tf_op jit(solution)/shard_map/all_to_all | solution.py:84
  716.9 397.3 %reduce-scatter.16.cloned.1.call-start = ((), (), s32[]{:S(2)}) async-start(), calls=%async_computation.17 | async-start | bytes 1081344
  885.9 232.7 %all-to-all-start.2 = ((bf16[4,64,3072]{2,1,0:T(8,128)(2,1)}), bf16[4,64,3072]{2,1,0:T(8,128)(2,1)}, u32[]{:S(2)}, u32[]{:S(2)}) async-start(bf16[4,64,3072]{2,1,0:T(8,128)(2,1)} %bitcast.286), calls=%async_computation.3 | async-start | bytes 3145728 | tf_op jit(solution)/shard_map/all_to_all | solution.py:84
  976.7 140.8 %collective-permute-start.17 = (bf16[128,2048]{1,0:T(8,128)(2,1)}, bf16[128,2048]{1,0:T(8,128)(2,1)S(1)}, u32[]{:S(2)}, u32[]{:S(2)}) collective-permute-start(bf16[128,2048]{1,0:T(8,128)(2,1)} %reduce-scatter.10.cloned.1.call-done), channel_id=1, source_target_pairs={{0,0},{4,1},{8,2},{12,3},{16,4},{20,5},{24,6},{28,7},{1,8},{5,9},{... | collective-permute-start | bytes 1572872 | tf_op jit(solution)/shard_map/ppermute | solution.py:207
  (73 other events, 797.1 us)
Sparse Core Ops, SparseCore 0:
  36.5 202.9 all-gather.5
  242.2 71.5 all-gather.7
  315.9 71.6 all-gather.9
  389.6 71.6 all-gather.11
  488.3 86.3 reduce-scatter.11
  588.6 86.5 reduce-scatter.13
  678.8 206.9 reduce-scatter.7
  889.5 87.1 reduce-scatter.9
  979.6 134.5 reduce-scatter.15
where the time goes:
time: 1140 us; the launch traced here: 1130 us
  waiting for transfers between devices  620 us (54%)
  matrix products  131 us (11%)
  blocking collectives  130 us (11%)
  local copies, waits for them, and re-layouts  127 us (11%)
  other arithmetic  78 us (7%)
  starting transfers between devices  26.5 us (2%)
  between operations  16.3 us (1%)
    reduce_scatter x4, waiting for transfers between devices, scatter_dp(): lax.psum_scatter(x.astype(bf16), 'dp', scatter_dimension=0, tiled=True)  216 us
    ppermute x16, waiting for transfers between devices, swap_seq(): return lax.ppermute(x, 'seq', [(i, i ^ bit) for i in range(size)])  150 us
    unnamed x10, waiting for transfers between devices  133 us
    dot_general x12, matrix products, dot(): return lax.dot_general(a, b, (dims, ((), ())), preferred_element_type=f32)  120 us
    all_gather x1, blocking collectives, local(): lax.all_gather(jnp.stack([norm1_gain, norm1_shift, norm2_gain, norm2_shif...  106 us
    all_gather x4, waiting for transfers between devices, gather_dp(): return lax.all_gather(x, 'dp', axis=0, tiled=True)  99.8 us
    unnamed x166, local copies, waits for them, and re-layouts  45.7 us
    all_to_all x1, blocking collectives, exchange_seq(): return lax.all_to_all(x, 'seq', 0, 0)  24.4 us
  transfers between devices with their start and end apart: 30, of which 17 were waited for; matrix products, arithmetic and copies ran while one was open for 24% of the time, Pallas kernels for 0%

commit v1 on v0

--- a/solution.py
+++ b/solution.py
@@ -11,6 +11,18 @@
 BOTH = ("dp", "seq")
 f32 = jnp.float32
 bf16 = jnp.bfloat16
+
+
+def gather_by_bits(array, axis, dim):
+    ways, here = (lax.axis_size(axis), lax.axis_index(axis))
+    grown, reach = (array, 1)
+    while reach < ways:
+        theirs = lax.ppermute(grown, axis, [(d, d ^ reach) for d in range(ways)])
+        mine_first = jnp.concatenate([grown, theirs], axis=dim)
+        theirs_first = jnp.concatenate([theirs, grown], axis=dim)
+        grown = jnp.where(here & reach == 0, mine_first, theirs_first)
+        reach = 2 * reach
+    return grown
 
 
 def layer_norm(rows, row_gain, row_shift):
@@ -85,7 +97,7 @@
 
 
 def gather_dp(x):
-    return lax.all_gather(x, "dp", axis=0, tiled=True)
+    return gather_by_bits(x, "dp", 0)
 
 
 def scatter_dp(x):

time: 1140 us -> 1620 us (1.42)
  waiting for transfers between devices: 620 us -> 1030 us
  other arithmetic: 78 us -> 103 us
  blocking collectives: 130 us -> 151 us
    ppermute x0 -> x12, waiting for transfers between devices: none -> 526 us  [gather_by_bits(): theirs = lax.ppermute(grown, axis, [(d, d ^ reach) for d in range(ways)])]
    all_gather x4 -> x0, waiting for transfers between devices: 99.8 us -> none  [gather_dp(): return lax.all_gather(x, 'dp', axis=0, tiled=True)]
    ppermute x16, waiting for transfers between devices: 150 us -> 115 us  [swap_seq(): return lax.ppermute(x, 'seq', [(i, i ^ bit) for i in range(size)])]
    select_n x0 -> x9, other arithmetic: none -> 25.1 us  [gather_by_bits(): grown = jnp.where(here & reach == 0, mine_first, theirs_first)]
    all_to_all x3, waiting for transfers between devices: 21.4 us -> 44.6 us  [exchange_seq(): return lax.all_to_all(x, 'seq', 0, 0)]
    all_gather x1, blocking collectives: 106 us -> 126 us  [local(): lax.all_gather(jnp.stack([norm1_gain, norm1_shift, norm2_gain, norm2_shif...]
    unnamed x166 -> x192, local copies, waits for them, and re-layouts: 45.7 us -> 47.8 us
    unnamed x10 -> x6, waiting for transfers between devices: 133 us -> 132 us
  transfers between devices with their start and end apart: 30 -> 38, of which waited for: 17 -> 22; matrix products, arithmetic and copies ran while one was open for 24% -> 14% of each run, Pallas kernels for 0% -> 0%
where the time goes in v1:
time: 1620 us; the launch traced here: 1610 us
  waiting for transfers between devices  1030 us (64%)
  blocking collectives  151 us (9%)
  matrix products  139 us (9%)
  local copies, waits for them, and re-layouts  128 us (8%)
  other arithmetic  103 us (6%)
  starting transfers between devices  40.6 us (3%)
  between operations  16.5 us (1%)
    ppermute x12, waiting for transfers between devices, gather_by_bits(): theirs = lax.ppermute(grown, axis, [(d, d ^ reach) for d in range(ways)])  526 us
    reduce_scatter x4, waiting for transfers between devices, scatter_dp(): lax.psum_scatter(x.astype(bf16), 'dp', scatter_dimension=0, tiled=True)  214 us
    unnamed x6, waiting for transfers between devices  132 us
    dot_general x12, matrix products, dot(): return lax.dot_general(a, b, (dims, ((), ())), preferred_element_type=f32)  128 us
    all_gather x1, blocking collectives, local(): lax.all_gather(jnp.stack([norm1_gain, norm1_shift, norm2_gain, norm2_shif...  126 us
    ppermute x16, waiting for transfers between devices, swap_seq(): return lax.ppermute(x, 'seq', [(i, i ^ bit) for i in range(size)])  115 us
    unnamed x192, local copies, waits for them, and re-layouts  47.8 us
    all_to_all x3, waiting for transfers between devices, exchange_seq(): return lax.all_to_all(x, 'seq', 0, 0)  44.6 us
  transfers between devices with their start and end apart: 38, of which 22 were waited for; matrix products, arithmetic and copies ran while one was open for 14% of the time, Pallas kernels for 0%

profile of v1, /device:TPU:0, one launch (start us, length us, event | category | flops | bytes accessed | tf_op | source)
XLA Modules:
  0.0 1610.1 jit_solution(9430246132014562789)
XLA Ops:
  11.9 24.1 %all_to_all.20 = bf16[4,64,3072]{2,1,0:T(8,128)(2,1)S(1)} all-to-all(bf16[4,64,3072]{2,1,0:T(8,128)(2,1)S(1)} %copy.198), channel_id=1, replica_groups=mesh['dp'=8,'seq'=4] {'seq'}, dimensions={0} | all-to-all | bytes 3145728 | tf_op jit(solution)/shard_map/all_to_all | solution.py:96
  37.5 34.3 %collective-permute-done.2 = bf16[256,3072]{1,0:T(8,128)(2,1)S(1)} collective-permute-done((bf16[256,3072]{1,0:T(8,128)(2,1)S(1)}, bf16[256,3072]{1,0:T(8,128)(2,1)S(1)}, u32[]{:S(2)}, u32[]{:S(2)}) %collective-permute-start.2) | collective-permute-done | bytes 1572896 | tf_op jit(solution)/shard_map/ppermute | solution.py:20
  77.6 126.5 %all-gather = bf16[32,64,4]{1,2,0:T(4,128)(2,1)S(1)} all-gather(bf16[1,64,4]{1,2,0:T(4,128)(2,1)S(1)} %maximum_bitcast_fusion.1), channel_id=1, replica_groups=mesh['dp'=8,'seq'=4] {'dp','seq'}, dimensions={0}, use_global_device_ids=true | all-gather | bytes 16896 | tf_op jit(solution)/shard_map/all_gather | solution.py:128
  204.0 9.9 maximum_select_fusion.1
  220.0 9.5 collective-permute-done.6
  232.4 10.8 collective-permute-done
  247.8 124.4 %collective-permute-done.7 = bf16[256,2048]{1,0:T(8,128)(2,1)} collective-permute-done((bf16[256,2048]{1,0:T(8,128)(2,1)S(1)}, bf16[256,2048]{1,0:T(8,128)(2,1)}, u32[]{:S(2)}, u32[]{:S(2)}) %collective-permute-start.7) | collective-permute-done | bytes 1048608 | tf_op jit(solution)/shard_map/ppermute | solution.py:20
  387.4 189.2 %collective-permute-done.8 = bf16[512,2048]{1,0:T(8,128)(2,1)S(1)} collective-permute-done((bf16[512,2048]{1,0:T(8,128)(2,1)S(1)}, bf16[512,2048]{1,0:T(8,128)(2,1)S(1)}, u32[]{:S(2)}, u32[]{:S(2)}) %collective-permute-start.8) | collective-permute-done | bytes 2097184 | tf_op jit(solution)/shard_map/ppermute | solution.py:20
  580.3 23.1 %fusion.23 = f32[1024,3072]{1,0:T(8,128)} fusion(bf16[1024,2048]{1,0:T(8,128)(2,1)} %bitcast.259, bf16[1024,3072]{1,0:T(8,128)(2,1)} %collective-permute-done.4, bf16[1024,3072]{1,0:T(8,128)(2,1)} %maximum_select_fusion.1, pred[]{:T(512)S(6)} %eq.11), kind=kOutput, calls=%fused_computation.73 | convolution fusion | flops 12941524992 | bytes 29360128 | tf_op jit(solution)/shard_map/dot_general | solution.py:58
  624.2 6.6 reshape.744
  630.8 7.3 copy.200
  686.2 22.7 %all-to-all-done.1 = bf16[4,64,1024]{2,1,0:T(8,128)(2,1)} async-done(((bf16[4,64,1024]{2,1,0:T(8,128)(2,1)}), bf16[4,64,1024]{2,1,0:T(8,128)(2,1)}, u32[]{:S(2)}, u32[]{:S(2)}) %all-to-all-start.1) | async-done | bytes 524320 | tf_op jit(solution)/shard_map/all_to_all | solution.py:96
  713.6 17.8 %collective-permute-done.21 = bf16[1,256,2048]{2,1,0:T(8,128)(2,1)} collective-permute-done((bf16[1,256,2048]{2,1,0:T(8,128)(2,1)}, bf16[1,256,2048]{2,1,0:T(8,128)(2,1)}, u32[]{:S(2)}, u32[]{:S(2)}) %collective-permute-start.21) | collective-permute-done | bytes 1048608 | tf_op jit(solution)/shard_map/ppermute | solution.py:67
  739.5 13.4 collective-permute-done.11
  753.3 8.4 collective-permute-done.14
  766.0 36.0 %collective-permute-done.17 = bf16[256,2048]{1,0:T(8,128)(2,1)S(1)} collective-permute-done((bf16[256,2048]{1,0:T(8,128)(2,1)S(1)}, bf16[256,2048]{1,0:T(8,128)(2,1)S(1)}, u32[]{:S(2)}, u32[]{:S(2)}) %collective-permute-start.17) | collective-permute-done | bytes 1048608 | tf_op jit(solution)/shard_map/ppermute | solution.py:20
  806.1 96.1 %collective-permute-done.15 = bf16[1024,1024]{1,0:T(8,128)(2,1)S(1)} collective-permute-done((bf16[1024,1024]{1,0:T(8,128)(2,1)S(1)}, bf16[1024,1024]{1,0:T(8,128)(2,1)S(1)}, u32[]{:S(2)}, u32[]{:S(2)}) %collective-permute-start.15) | collective-permute-done | bytes 2097184 | tf_op jit(solution)/shard_map/ppermute | solution.py:20
  902.2 14.8 multiply_convert_fusion
  917.0 28.5 %collective-permute-done.18 = bf16[512,2048]{1,0:T(8,128)(2,1)S(1)} collective-permute-done((bf16[512,2048]{1,0:T(8,128)(2,1)S(1)}, bf16[512,2048]{1,0:T(8,128)(2,1)S(1)}, u32[]{:S(2)}, u32[]{:S(2)}) %collective-permute-start.18) | collective-permute-done | bytes 2097184 | tf_op jit(solution)/shard_map/ppermute | solution.py:20
  946.7 9.9 add_convert_fusion.2
  964.4 8.6 fusion.60
  990.4 18.6 %collective-permute-done.24 = bf16[1,256,2048]{2,1,0:T(8,128)(2,1)S(1)} collective-permute-done((bf16[1,256,2048]{2,1,0:T(8,128)(2,1)S(1)}, bf16[1,256,2048]{2,1,0:T(8,128)(2,1)S(1)}, u32[]{:S(2)}, u32[]{:S(2)}) %collective-permute-start.24) | collective-permute-done | bytes 1048608 | tf_op jit(solution)/shard_map/ppermute | solution.py:67
  1009.8 21.3 %collective-permute-done.20 = bf16[1,256,2048]{2,1,0:T(8,128)(2,1)S(1)} collective-permute-done((bf16[1,256,2048]{2,1,0:T(8,128)(2,1)S(1)}, bf16[1,256,2048]{2,1,0:T(8,128)(2,1)S(1)}, u32[]{:S(2)}, u32[]{:S(2)}) %collective-permute-start.20) | collective-permute-done | bytes 1048608 | tf_op jit(solution)/shard_map/ppermute | solution.py:67
  1036.9 23.3 %collective-permute-done.25 = bf16[1,256,2048]{2,1,0:T(8,128)(2,1)S(1)} collective-permute-done((bf16[1,256,2048]{2,1,0:T(8,128)(2,1)S(1)}, bf16[1,256,2048]{2,1,0:T(8,128)(2,1)S(1)}, u32[]{:S(2)}, u32[]{:S(2)}) %collective-permute-start.25) | collective-permute-done | bytes 1048608 | tf_op jit(solution)/shard_map/ppermute | solution.py:67
  1090.1 6.4 copy.235
  1131.0 16.0 convolution_convert_fusion
  1147.0 6.4 copy.241
  1162.5 20.5 %fusion.22 = f32[1024,2048]{1,0:T(8,128)S(1)} fusion(bf16[1024,3072]{1,0:T(8,128)(2,1)} %copy-done.54, bf16[1024,3072]{1,0:T(8,128)(2,1)} %collective-permute-done.4, bf16[1024,3072]{1,0:T(8,128)(2,1)} %maximum_select_fusion.1, pred[]{:T(512)S(6)} %eq.11), kind=kOutput, calls=%fused_computation.72 | convolution fusion | flops 12941524992 | bytes 27262976 | tf_op jit(solution)/shard_map/dot_general | solution.py:58
  1200.9 21.9 %all-to-all-done.3 = bf16[4,64,1024]{2,1,0:T(8,128)(2,1)} async-done(((bf16[4,64,1024]{2,1,0:T(8,128)(2,1)}), bf16[4,64,1024]{2,1,0:T(8,128)(2,1)}, u32[]{:S(2)}, u32[]{:S(2)}) %all-to-all-start.3) | async-done | bytes 524320 | tf_op jit(solution)/shard_map/all_to_all | solution.py:96
  1234.8 131.6 %reduce-scatter.8.cloned.1.call-done = bf16[256,3072]{1,0:T(8,128)(2,1)} async-done(((bf16[2048,3072]{1,0:T(8,128)(2,1)}), bf16[256,3072]{1,0:T(8,128)(2,1)}) %reduce-scatter.8.cloned.1.call-update) | async-done | bytes 1572880 | tf_op jit(solution)/shard_map/reduce_scatter | solution.py:104
  1374.8 82.2 %reduce-scatter.10.cloned.1.call-done = bf16[128,2048]{1,0:T(8,128)(2,1)} async-done(((bf16[1024,2048]{1,0:T(8,128)(2,1)}), bf16[128,2048]{1,0:T(8,128)(2,1)}) %reduce-scatter.10.cloned.1.call-update) | async-done | bytes 524304 | tf_op jit(solution)/shard_map/reduce_scatter | solution.py:104
  1462.0 132.4 %reduce-scatter.16.cloned.1.call-done = f32[64,4]{1,0:T(8,128)} async-done(((f32[2048,4]{1,0:T(8,128)}), f32[64,4]{1,0:T(8,128)}) %reduce-scatter.16.cloned.1.call-update) | async-done | bytes 1040
  (399 shorter events, 291.2 us)
Async XLA Ops:
  36.0 35.8 %collective-permute-start.2 = (bf16[256,3072]{1,0:T(8,128)(2,1)S(1)}, bf16[256,3072]{1,0:T(8,128)(2,1)S(1)}, u32[]{:S(2)}, u32[]{:S(2)}) collective-permute-start(bf16[256,3072]{1,0:T(8,128)(2,1)S(1)} %bitcast.248), channel_id=1, source_target_pairs={{0,4},{4,0},{8,12},{12,8},{16,20},{20,16},{24,28},{28,24},{1,5},{5... | collective-permute-start | bytes 4718600 | tf_op jit(solution)/shard_map/ppermute | solution.py:20
  74.3 129.8 %collective-permute-start.3 = (bf16[512,3072]{1,0:T(8,128)(2,1)}, bf16[512,3072]{1,0:T(8,128)(2,1)}, u32[]{:S(2)}, u32[]{:S(2)}) collective-permute-start(bf16[512,3072]{1,0:T(8,128)(2,1)} %maximum_select_fusion.9), channel_id=1, source_target_pairs={{0,8},{4,12},{8,0},{12,4},{16,24},{20,28},{24,16},{28,20},{1,9},{5... | collective-permute-start | bytes 9437192 | tf_op jit(solution)/shard_map/ppermute | solution.py:20
  75.8 139.4 %collective-permute-start.5 = (bf16[128,2048]{1,0:T(8,128)(2,1)}, bf16[128,2048]{1,0:T(8,128)(2,1)S(1)}, u32[]{:S(2)}, u32[]{:S(2)}) collective-permute-start(bf16[128,2048]{1,0:T(8,128)(2,1)} %param.17), channel_id=1, source_target_pairs={{0,0},{1,4},{2,8},{3,12},{4,16},{5,20},{6,24},{7,28},{8,1},{9,5},{... | collective-permute-start | bytes 1572872 | tf_op jit(solution)/shard_map/ppermute | solution.py:142
  214.0 366.3 %collective-permute-start.4 = (bf16[1024,3072]{1,0:T(8,128)(2,1)}, bf16[1024,3072]{1,0:T(8,128)(2,1)}, u32[]{:S(2)}, u32[]{:S(2)}) collective-permute-start(bf16[1024,3072]{1,0:T(8,128)(2,1)} %maximum_select_fusion.1), channel_id=1, source_target_pairs={{0,16},{4,20},{8,24},{12,28},{16,0},{20,4},{24,8},{28,12},{1,17},{... | collective-permute-start | bytes 18874376 | tf_op jit(solution)/shard_map/ppermute | solution.py:20
  217.4 25.9 %collective-permute-start = (bf16[1,256,2048]{2,1,0:T(8,128)(2,1)}, bf16[1,256,2048]{2,1,0:T(8,128)(2,1)S(1)}, u32[]{:S(2)}, u32[]{:S(2)}) collective-permute-start(bf16[1,256,2048]{2,1,0:T(8,128)(2,1)} %get-tuple-element.56), channel_id=1, source_target_pairs={{0,2},{1,3},{2,0},{3,1},{4,6},{5,7},{6,4},{7,5},{8,10},{9,11},{10,... | collective-permute-start | bytes 3145736 | tf_op jit(solution)/shard_map/ppermute | solution.py:67
  231.0 141.2 %collective-permute-start.7 = (bf16[256,2048]{1,0:T(8,128)(2,1)S(1)}, bf16[256,2048]{1,0:T(8,128)(2,1)}, u32[]{:S(2)}, u32[]{:S(2)}) collective-permute-start(bf16[256,2048]{1,0:T(8,128)(2,1)S(1)} %maximum_select_fusion.23), channel_id=1, source_target_pairs={{0,8},{4,12},{8,0},{12,4},{16,24},{20,28},{24,16},{28,20},{1,9},{5... | collective-permute-start | bytes 3145736 | tf_op jit(solution)/shard_map/ppermute | solution.py:20
  246.5 135.7 %collective-permute-start.1 = (bf16[2,256,2048]{2,1,0:T(8,128)(2,1)}, bf16[2,256,2048]{2,1,0:T(8,128)(2,1)}, u32[]{:S(2)}, u32[]{:S(2)}) collective-permute-start(bf16[2,256,2048]{2,1,0:T(8,128)(2,1)} %maximum_select_fusion.12), channel_id=1, source_target_pairs={{0,1},{1,0},{2,3},{3,2},{4,5},{5,4},{6,7},{7,6},{8,9},{9,8},{10,11... | collective-permute-start | bytes 6291464 | tf_op jit(solution)/shard_map/ppermute | solution.py:67
  374.6 202.0 %collective-permute-start.8 = (bf16[512,2048]{1,0:T(8,128)(2,1)S(1)}, bf16[512,2048]{1,0:T(8,128)(2,1)S(1)}, u32[]{:S(2)}, u32[]{:S(2)}) collective-permute-start(bf16[512,2048]{1,0:T(8,128)(2,1)S(1)} %maximum_select_fusion.14), channel_id=1, source_target_pairs={{0,16},{4,20},{8,24},{12,28},{16,0},{20,4},{24,8},{28,12},{1,17},{... | collective-permute-start | bytes 6291464 | tf_op jit(solution)/shard_map/ppermute | solution.py:20
  677.1 31.8 %collective-permute-start.10 = (bf16[1,256,2048]{2,1,0:T(8,128)(2,1)S(1)}, bf16[1,256,2048]{2,1,0:T(8,128)(2,1)}, u32[]{:S(2)}, u32[]{:S(2)}) collective-permute-start(bf16[1,256,2048]{2,1,0:T(8,128)(2,1)S(1)} %dynamic-slice_convert_fusion.4), channel_id=1, source_target_pairs={{0,2},{1,3},{2,0},{3,1},{4,6},{5,7},{6,4},{7,5},{8,10},{9,11},{10,... | collective-permute-start | bytes 3145736 | tf_op jit(solution)/shard_map/ppermute | solution.py:67
  680.0 28.8 %all-to-all-start.1 = ((bf16[4,64,1024]{2,1,0:T(8,128)(2,1)}), bf16[4,64,1024]{2,1,0:T(8,128)(2,1)}, u32[]{:S(2)}, u32[]{:S(2)}) async-start(bf16[4,64,1024]{2,1,0:T(8,128)(2,1)} %reshape.749), calls=%async_computation.1 | async-start | bytes 1048576 | tf_op jit(solution)/shard_map/all_to_all | solution.py:96
  684.2 508.5 %reduce-scatter.12.cloned.1.call-start = ((), (), s32[]{:S(2)}) async-start(), calls=%async_computation.11 | async-start | bytes 4718592 | tf_op jit(solution)/shard_map/reduce_scatter | solution.py:104
  684.3 51.6 %collective-permute-start.16 = (bf16[128,2048]{1,0:T(8,128)(2,1)}, bf16[128,2048]{1,0:T(8,128)(2,1)}, u32[]{:S(2)}, u32[]{:S(2)}) collective-permute-start(bf16[128,2048]{1,0:T(8,128)(2,1)} %param.21), channel_id=1, source_target_pairs={{0,4},{4,0},{8,12},{12,8},{16,20},{20,16},{24,28},{28,24},{1,5},{5... | collective-permute-start | bytes 1572872 | tf_op jit(solution)/shard_map/ppermute | solution.py:20
  684.3 47.0 %collective-permute-start.21 = (bf16[1,256,2048]{2,1,0:T(8,128)(2,1)}, bf16[1,256,2048]{2,1,0:T(8,128)(2,1)}, u32[]{:S(2)}, u32[]{:S(2)}) collective-permute-start(bf16[1,256,2048]{2,1,0:T(8,128)(2,1)} %bitcast.42), channel_id=1, source_target_pairs={{0,2},{1,3},{2,0},{3,1},{4,6},{5,7},{6,4},{7,5},{8,10},{9,11},{10,... | collective-permute-start | bytes 3145736 | tf_op jit(solution)/shard_map/ppermute | solution.py:67
  708.9 25.2 %collective-permute-start.13 = (bf16[256,1024]{1,0:T(8,128)(2,1)}, bf16[256,1024]{1,0:T(8,128)(2,1)S(1)}, u32[]{:S(2)}, u32[]{:S(2)}) collective-permute-start(bf16[256,1024]{1,0:T(8,128)(2,1)} %bitcast.37), channel_id=1, source_target_pairs={{0,4},{4,0},{8,12},{12,8},{16,20},{20,16},{24,28},{28,24},{1,5},{5... | collective-permute-start | bytes 1572872 | tf_op jit(solution)/shard_map/ppermute | solution.py:20
  712.1 40.8 %collective-permute-start.11 = (bf16[1,256,2048]{2,1,0:T(8,128)(2,1)S(1)}, bf16[1,256,2048]{2,1,0:T(8,128)(2,1)S(1)}, u32[]{:S(2)}, u32[]{:S(2)}) collective-permute-start(bf16[1,256,2048]{2,1,0:T(8,128)(2,1)S(1)} %fusion.127), channel_id=1, source_target_pairs={{0,2},{1,3},{2,0},{3,1},{4,6},{5,7},{6,4},{7,5},{8,10},{9,11},{10,... | collective-permute-start | bytes 3145736 | tf_op jit(solution)/shard_map/ppermute | solution.py:67
  734.0 69.3 %collective-permute-start.22 = (bf16[2,256,2048]{2,1,0:T(8,128)(2,1)S(1)}, bf16[2,256,2048]{2,1,0:T(8,128)(2,1)S(1)}, u32[]{:S(2)}, u32[]{:S(2)}) collective-permute-start(bf16[2,256,2048]{2,1,0:T(8,128)(2,1)S(1)} %maximum_select_fusion.19), channel_id=1, source_target_pairs={{0,1},{1,0},{2,3},{3,2},{4,5},{5,4},{6,7},{7,6},{8,9},{9,8},{10,11... | collective-permute-start | bytes 6291464 | tf_op jit(solution)/shard_map/ppermute | solution.py:67
  735.7 26.0 %collective-permute-start.14 = (bf16[512,1024]{1,0:T(8,128)(2,1)S(1)}, bf16[512,1024]{1,0:T(8,128)(2,1)S(1)}, u32[]{:S(2)}, u32[]{:S(2)}) collective-permute-start(bf16[512,1024]{1,0:T(8,128)(2,1)S(1)} %maximum_select_fusion.24), channel_id=1, source_target_pairs={{0,8},{4,12},{8,0},{12,4},{16,24},{20,28},{24,16},{28,20},{1,9},{5... | collective-permute-start | bytes 3145736 | tf_op jit(solution)/shard_map/ppermute | solution.py:20
  737.4 64.7 %collective-permute-start.17 = (bf16[256,2048]{1,0:T(8,128)(2,1)S(1)}, bf16[256,2048]{1,0:T(8,128)(2,1)S(1)}, u32[]{:S(2)}, u32[]{:S(2)}) collective-permute-start(bf16[256,2048]{1,0:T(8,128)(2,1)S(1)} %maximum_select_fusion.25), channel_id=1, source_target_pairs={{0,8},{4,12},{8,0},{12,4},{16,24},{20,28},{24,16},{28,20},{1,9},{5... | collective-permute-start | bytes 3145736 | tf_op jit(solution)/shard_map/ppermute | solution.py:20
  753.3 51.8 %collective-permute-start.12 = (bf16[2,256,2048]{2,1,0:T(8,128)(2,1)S(1)}, bf16[2,256,2048]{2,1,0:T(8,128)(2,1)S(1)}, u32[]{:S(2)}, u32[]{:S(2)}) collective-permute-start(bf16[2,256,2048]{2,1,0:T(8,128)(2,1)S(1)} %maximum_select_fusion.15), channel_id=1, source_target_pairs={{0,1},{1,0},{2,3},{3,2},{4,5},{5,4},{6,7},{7,6},{8,9},{9,8},{10,11... | collective-permute-start | bytes 6291464 | tf_op jit(solution)/shard_map/ppermute | solution.py:67
  762.8 139.4 %collective-permute-start.15 = (bf16[1024,1024]{1,0:T(8,128)(2,1)S(1)}, bf16[1024,1024]{1,0:T(8,128)(2,1)S(1)}, u32[]{:S(2)}, u32[]{:S(2)}) collective-permute-start(bf16[1024,1024]{1,0:T(8,128)(2,1)S(1)} %maximum_select_fusion.17), channel_id=1, source_target_pairs={{0,16},{4,20},{8,24},{12,28},{16,0},{20,4},{24,8},{28,12},{1,17},{... | collective-permute-start | bytes 6291464 | tf_op jit(solution)/shard_map/ppermute | solution.py:20
  803.0 142.4 %collective-permute-start.18 = (bf16[512,2048]{1,0:T(8,128)(2,1)S(1)}, bf16[512,2048]{1,0:T(8,128)(2,1)S(1)}, u32[]{:S(2)}, u32[]{:S(2)}) collective-permute-start(bf16[512,2048]{1,0:T(8,128)(2,1)S(1)} %maximum_select_fusion.18), channel_id=1, source_target_pairs={{0,16},{4,20},{8,24},{12,28},{16,0},{20,4},{24,8},{28,12},{1,17},{... | collective-permute-start | bytes 6291464 | tf_op jit(solution)/shard_map/ppermute | solution.py:20
  964.2 234.6 %reduce-scatter.14.cloned.1.call-start = ((), (), s32[]{:S(2)}) async-start(), calls=%async_computation.12 | async-start | bytes 4718592 | tf_op jit(solution)/shard_map/reduce_scatter | solution.py:104
  983.0 26.0 %collective-permute-start.24 = (bf16[1,256,2048]{2,1,0:T(8,128)(2,1)S(1)}, bf16[1,256,2048]{2,1,0:T(8,128)(2,1)S(1)}, u32[]{:S(2)}, u32[]{:S(2)}) collective-permute-start(bf16[1,256,2048]{2,1,0:T(8,128)(2,1)S(1)} %dynamic-slice_convert_fusion.2), channel_id=1, source_target_pairs={{0,2},{1,3},{2,0},{3,1},{4,6},{5,7},{6,4},{7,5},{8,10},{9,11},{10,... | collective-permute-start | bytes 3145736 | tf_op jit(solution)/shard_map/ppermute | solution.py:67
  988.9 42.2 %collective-permute-start.20 = (bf16[1,256,2048]{2,1,0:T(8,128)(2,1)S(1)}, bf16[1,256,2048]{2,1,0:T(8,128)(2,1)S(1)}, u32[]{:S(2)}, u32[]{:S(2)}) collective-permute-start(bf16[1,256,2048]{2,1,0:T(8,128)(2,1)S(1)} %dynamic-slice_convert_fusion.3), channel_id=1, source_target_pairs={{0,2},{1,3},{2,0},{3,1},{4,6},{5,7},{6,4},{7,5},{8,10},{9,11},{10,... | collective-permute-start | bytes 3145736 | tf_op jit(solution)/shard_map/ppermute | solution.py:67
  1035.4 24.8 %collective-permute-start.25 = (bf16[1,256,2048]{2,1,0:T(8,128)(2,1)S(1)}, bf16[1,256,2048]{2,1,0:T(8,128)(2,1)S(1)}, u32[]{:S(2)}, u32[]{:S(2)}) collective-permute-start(bf16[1,256,2048]{2,1,0:T(8,128)(2,1)S(1)} %fusion.125), channel_id=1, source_target_pairs={{0,2},{1,3},{2,0},{3,1},{4,6},{5,7},{6,4},{7,5},{8,10},{9,11},{10,... | collective-permute-start | bytes 3145736 | tf_op jit(solution)/shard_map/ppermute | solution.py:67
  1068.6 297.8 %reduce-scatter.8.cloned.1.call-start = ((), (), s32[]{:S(2)}) async-start(), calls=%async_computation.9 | async-start | bytes 14155776 | tf_op jit(solution)/shard_map/reduce_scatter | solution.py:104
  1147.0 310.0 %reduce-scatter.10.cloned.1.call-start = ((), (), s32[]{:S(2)}) async-start(), calls=%async_computation.10 | async-start | bytes 4718592 | tf_op jit(solution)/shard_map/reduce_scatter | solution.py:104
  1191.5 36.9 %collective-permute-start.28 = (bf16[1,256,2048]{2,1,0:T(8,128)(2,1)}, bf16[1,256,2048]{2,1,0:T(8,128)(2,1)}, u32[]{:S(2)}, u32[]{:S(2)}) collective-permute-start(bf16[1,256,2048]{2,1,0:T(8,128)(2,1)} %dynamic-slice_convert_fusion.1), channel_id=1, source_target_pairs={{0,2},{1,3},{2,0},{3,1},{4,6},{5,7},{6,4},{7,5},{8,10},{9,11},{10,... | collective-permute-start | bytes 3145736 | tf_op jit(solution)/shard_map/ppermute | solution.py:67
  1192.7 30.2 %all-to-all-start.3 = ((bf16[4,64,1024]{2,1,0:T(8,128)(2,1)}), bf16[4,64,1024]{2,1,0:T(8,128)(2,1)}, u32[]{:S(2)}, u32[]{:S(2)}) async-start(bf16[4,64,1024]{2,1,0:T(8,128)(2,1)} %bitcast.284), calls=%async_computation.6 | async-start | bytes 1048576 | tf_op jit(solution)/shard_map/all_to_all | solution.py:96
  1196.8 397.5 %reduce-scatter.16.cloned.1.call-start = ((), (), s32[]{:S(2)}) async-start(), calls=%async_computation.13 | async-start | bytes 1081344
  1366.5 232.4 %all-to-all-start.2 = ((bf16[4,64,3072]{2,1,0:T(8,128)(2,1)}), bf16[4,64,3072]{2,1,0:T(8,128)(2,1)}, u32[]{:S(2)}, u32[]{:S(2)}) async-start(bf16[4,64,3072]{2,1,0:T(8,128)(2,1)} %bitcast.281), calls=%async_computation.3 | async-start | bytes 3145728 | tf_op jit(solution)/shard_map/all_to_all | solution.py:96
  1457.0 140.7 %collective-permute-start.29 = (bf16[128,2048]{1,0:T(8,128)(2,1)}, bf16[128,2048]{1,0:T(8,128)(2,1)S(1)}, u32[]{:S(2)}, u32[]{:S(2)}) collective-permute-start(bf16[128,2048]{1,0:T(8,128)(2,1)} %reduce-scatter.10.cloned.1.call-done), channel_id=1, source_target_pairs={{0,0},{4,1},{8,2},{12,3},{16,4},{20,5},{24,6},{28,7},{1,8},{5,9},{... | collective-permute-start | bytes 1572872 | tf_op jit(solution)/shard_map/ppermute | solution.py:219
  (94 other events, 2441.6 us)
Sparse Core Ops, SparseCore 0:
  964.3 86.8 reduce-scatter.11
  1068.8 87.0 reduce-scatter.13
  1159.4 206.9 reduce-scatter.7
  1369.9 87.0 reduce-scatter.9
  1459.8 134.5 reduce-scatter.15
